TPU v7x, 256 devices: a whole 4x4x8 slice. The times are simulated.
256 devices in a mesh: pipe: 4 (over y_hi, core), ctx: 8 (over y_lo, x), tp: 8 (over z).
Axes of the slice: x: 4, y: 4 (y_hi: 2, y_lo: 2; y = y_hi * 2 + y_lo), z: 8, core: 2. Of those that a mesh axis runs over, the one named last changes fastest.
Arguments:
- section_input: bfloat16 [4, 1024, 8192], P('pipe', 'tp', 'ctx'), may hold values from -42 to 42, as said below
- norm_gain: bfloat16 [4, 8192], P('pipe', 'ctx'), may hold values from 0.099609375 to 1.8984375
- in_weight: bfloat16 [4, 8192, 3, 8192], P('pipe', 'ctx', None, 'tp'), may hold values from -0.0625 to 0.0625
- qkv_filters: bfloat16 [4, 3, 128, 8192], P('pipe', None, None, 'tp'), may hold values from -0.5 to 0.5
- mix_filter: bfloat16 [4, 128, 8192], P('pipe', None, 'tp'), may hold values from -0.5 to 0.5
- out_weight: bfloat16 [4, 8192, 8192], P('pipe', 'tp', 'ctx'), may hold values from -0.0625 to 0.0625
Outputs:
- handed: bfloat16 [4, 1024, 8192], P('pipe', 'tp', 'ctx')
Inputs may be any that keep to these rules, and one draw needn't show every extreme that they name: `section_input`: Real-valued activations with position and feature scales of order one.
All inputs are finite; a program needn't handle non-finite values.
Results may differ from a plain program's by a relative error of at most 0.029.
Values may be sent and summed in bfloat16 or wider, within the bound.
No kernel may reach another device: no remote copies, remote signals or barrier semaphores. Data moves between devices by JAX's collectives and lax.ppermute only.
A program may use at most 128 MiB of HBM per device.

v0:
```python
import jax
import jax.numpy as jnp
from jax import lax
from jax.sharding import PartitionSpec as P

D = 8192
NORM_EPS = 1e-05


def passed_along(value, axis, steps):
    count = lax.axis_size(axis)
    first, last = (max(0, -steps), min(count, count - steps))
    return lax.ppermute(value, axis, [(source, source + steps) for source in range(first, last)])


def shifted(value, axis, steps):
    count = lax.axis_size(axis)
    pairs = [(source, (source + steps) % count) for source in range(count)]
    return lax.ppermute(value, axis, pairs)


def causal_mix(padded, tap_weights):
    channels = tap_weights.shape[1]
    kernel = tap_weights[::-1][:, None, :]
    result = lax.conv_general_dilated(
        padded[None],
        kernel,
        (1,),
        "VALID",
        dimension_numbers=("NWC", "WIO", "NWC"),
        feature_group_count=channels,
        precision=lax.Precision.HIGHEST,
    )
    return result[0]


def on_device(section_input, norm_gain, in_weight, qkv_filters, mix_filter, out_weight):
    incoming = section_input[0].astype(jnp.float32)
    squares = lax.psum(jnp.sum(incoming * incoming, axis=1), "ctx")
    normed = (
        incoming * lax.rsqrt(squares[:, None] / D + NORM_EPS) * norm_gain[0].astype(jnp.float32)
    ).astype(jnp.bfloat16)
    gathered = lax.all_gather(normed, "tp", axis=0, tiled=True)
    width_in = in_weight.shape[1]
    channels = in_weight.shape[3]
    weight_in = in_weight[0].reshape(width_in, 3 * channels)
    weight_out = out_weight[0]
    tap_count = qkv_filters.shape[2]
    filters_qkv = qkv_filters[0].astype(jnp.float32)
    filters_mix = mix_filter[0].astype(jnp.float32)
    total_rows = gathered.shape[0]
    seg_rows = total_rows // lax.axis_size("ctx")
    projected = lax.psum_scatter(
        jnp.dot(gathered, weight_in, preferred_element_type=jnp.float32).astype(jnp.bfloat16),
        "ctx",
        scatter_dimension=0,
        tiled=True,
    )
    prior_rows = passed_along(projected[seg_rows - (tap_count - 1) :], "ctx", 1)
    padded = jnp.concatenate([prior_rows, projected], 0).astype(jnp.float32)
    table_qkv = jnp.transpose(filters_qkv, (1, 0, 2)).reshape(tap_count, 3 * channels)
    filtered = causal_mix(padded, table_qkv).reshape(seg_rows, 3, channels)
    product = (filtered[:, 1] * filtered[:, 2]).astype(jnp.bfloat16)
    prior_prod = passed_along(product[seg_rows - (tap_count - 1) :], "ctx", 1)
    mixed_sig = causal_mix(
        jnp.concatenate([prior_prod, product], 0).astype(jnp.float32), filters_mix
    )
    gated_out = (filtered[:, 0] * mixed_sig).astype(jnp.bfloat16)
    partial_value = jnp.dot(
        lax.all_gather(gated_out, "ctx", axis=0, tiled=True),
        weight_out,
        preferred_element_type=jnp.float32,
    )
    summed = lax.psum_scatter(
        partial_value.astype(jnp.bfloat16), "tp", scatter_dimension=0, tiled=True
    ).astype(jnp.float32)
    block_out = (incoming + summed).astype(jnp.bfloat16)
    handed = shifted(block_out, "pipe", 1)
    return handed[None]


def solution(mesh):
    return jax.shard_map(
        on_device,
        mesh=mesh,
        in_specs=(
            P("pipe", "tp", "ctx"),
            P("pipe", "ctx"),
            P("pipe", "ctx", None, "tp"),
            P("pipe", None, None, "tp"),
            P("pipe", None, "tp"),
            P("pipe", "tp", "ctx"),
        ),
        out_specs=P("pipe", "tp", "ctx"),
        check_vma=False,
    )
```

profile of v0, /device:TPU:1, one launch (start us, length us, event | category | flops | bytes accessed | tf_op | source)
XLA Modules:
  0.0 338.4 jit_solution(3435110821669046357)
XLA Ops:
  6.5 0.8 mul.40
  7.4 1.1 fusion.7
  8.5 16.8 %psum.7 = f32[128]{0:T(128)S(1)} all-reduce(f32[128]{0:T(128)S(1)} %fusion.7), channel_id=1, replica_groups=mesh['pipe'=4,'ctx'=8,'tp'=8] {'ctx'}, use_global_device_ids=true, to_apply=%region_1.0 | all-reduce | flops 128 | bytes 1024 | tf_op jit(solution)/shard_map/psum | solution.py:39
  25.2 1.8 fusion.9
  27.1 8.7 %copy.12 = bf16[1,1024,3,1024]{1,3,2,0:T(8,128)(2,1)} copy(bf16[1,1024,3,1024]{3,1,2,0:T(8,128)(2,1)} %param.8) | data formatting | bytes 12582912 | tf_op args[2]
  35.8 32.1 %all-gather.3.cloned.1.call-done = bf16[1024,1024]{1,0:T(8,128)(2,1)} async-done(((bf16[128,1024]{1,0:T(8,128)(2,1)}), bf16[1024,1024]{1,0:T(8,128)(2,1)}) %all-gather.3.cloned.1.call-update) | async-done | bytes 2097168 | tf_op jit(solution)/shard_map/all_gather | solution.py:43
  67.9 11.3 %convolution_convert_fusion = bf16[1024,3072]{1,0:T(8,128)(2,1)} fusion(bf16[1024,1024]{1,0:T(8,128)(2,1)} %all-gather.3.cloned.1.call-done, bf16[1024,3072]{0,1:T(8,128)(2,1)} %bitcast.43), kind=kOutput, calls=%fused_computation | convolution fusion | flops 6445596672 | bytes 14680064 | tf_op jit(solution)/shard_map/dot_general | solution.py:54
  79.2 78.2 %reduce-scatter.3.cloned.1.call-done = bf16[128,3072]{1,0:T(8,128)(2,1)} async-done(((bf16[1024,3072]{1,0:T(8,128)(2,1)}), bf16[128,3072]{1,0:T(8,128)(2,1)}) %reduce-scatter.3.cloned.1.call-update) | async-done | bytes 786448 | tf_op jit(solution)/shard_map/reduce_scatter | solution.py:53
  157.5 2.2 slice.24
  159.7 2.2 collective-permute-start
  161.8 1.5 copy.13
  163.4 1.3 bitcast_convert_fusion
  164.6 13.3 %rev.6 = f32[128,3072]{0,1:T(8,128)} reverse(f32[128,3072]{0,1:T(8,128)} %bitcast.45), dimensions={0} | reverse | bytes 3145728 | tf_op jit(solution)/shard_map/rev | solution.py:24
  177.9 4.6 %copy.15 = f32[128,1,3072]{2,1,0:T(1,128)} copy(f32[128,1,3072]{0,2,1:T(8,128)} %bitcast.46) | data formatting | bytes 3145728 | tf_op jit(solution)/shard_map/broadcast_in_dim | solution.py:24
  182.5 1.5 maximum_bitcast_fusion
  184.2 17.5 %fusion = f32[1,128,3072]{2,0,1:T(1,128)} fusion(f32[128,1,3072]{2,1,0:T(1,128)S(1)} %copy-done.3, bf16[1,255,3072]{2,1,0:T(8,128)(2,1)S(1)} %maximum_bitcast_fusion), kind=kOutput, calls=%fused_computation.1 | convolution fusion | flops 603979776 | bytes 4712448 | tf_op jit(solution)/shard_map/conv_general_dilated | solution.py:25
  201.7 4.4 %copy.16 = f32[1,128,3072]{1,2,0:T(8,128)} copy(f32[1,128,3072]{2,0,1:T(1,128)} %fusion) | data formatting | bytes 3145728 | tf_op jit(solution)/shard_map/conv_general_dilated | solution.py:25
  206.1 2.3 fusion.15
  208.4 0.8 slice_bitcast_fusion
  209.2 2.3 collective-permute-start.1
  211.5 2.7 rev.7
  214.2 1.2 copy.24
  215.7 1.2 maximum_bitcast_fusion.1
  216.9 2.1 copy.19
  219.0 7.3 %fusion.13 = f32[1,128,1024]{2,0,1:T(1,128)S(1)} fusion(bf16[1,255,1024]{2,0,1:T(2,128)(2,1)} %copy.19, f32[128,1,1024]{2,0,1:T(8,128)} %bitcast.48), kind=kOutput, calls=%fused_computation.20 | convolution fusion | flops 201326592 | bytes 1570816 | tf_op jit(solution)/shard_map/conv_general_dilated | solution.py:25
  226.3 0.8 fusion.12
  227.2 43.2 %all-gather.5.cloned.1.call-done = bf16[1024,1024]{1,0:T(8,128)(2,1)} async-done(((bf16[128,1024]{1,0:T(8,128)(2,1)}), bf16[1024,1024]{1,0:T(8,128)(2,1)}) %all-gather.5.cloned.1.call-update) | async-done | bytes 2097168 | tf_op jit(solution)/shard_map/all_gather | solution.py:70
  270.4 5.3 %fusion.4 = bf16[1024,1024]{1,0:T(8,128)(2,1)} fusion(bf16[1024,1024]{1,0:T(8,128)(2,1)} %all-gather.5.cloned.1.call-done, bf16[1,1024,1024]{2,1,0:T(8,128)(2,1)S(1)} %copy-done), kind=kOutput, calls=%fused_computation.5 | convolution fusion | flops 2148532224 | bytes 6291456 | tf_op jit(solution)/shard_map/dot_general | solution.py:69
  275.7 43.1 %reduce-scatter.5.cloned.1.call-done = bf16[128,1024]{1,0:T(8,128)(2,1)} async-done(((bf16[1024,1024]{1,0:T(8,128)(2,1)}), bf16[128,1024]{1,0:T(8,128)(2,1)}) %reduce-scatter.5.cloned.1.call-update) | async-done | bytes 262160 | tf_op jit(solution)/shard_map/reduce_scatter | solution.py:74
  318.8 1.0 fusion.10
  319.8 8.0 %collective-permute-start.2 = (bf16[128,1024]{1,0:T(8,128)(2,1)S(1)}, bf16[128,1024]{1,0:T(8,128)(2,1)S(1)}, u32[]{:S(2)}, u32[]{:S(2)}) collective-permute-start(bf16[128,1024]{1,0:T(8,128)(2,1)S(1)} %fusion.10), channel_id=1, source_target_pairs={{0,64},{64,128},{128,192},{192,0},{1,65},{65,129},{129,193},{193,1... | collective-permute-start | bytes 786440 | tf_op jit(solution)/shard_map/ppermute | solution.py:19
  327.8 3.3 collective-permute-done.2
  (23 shorter events, 1.4 us)
Async XLA Ops:
  6.5 263.9 %copy-start = (bf16[1,1024,1024]{2,1,0:T(8,128)(2,1)S(1)}, bf16[1,1024,1024]{2,1,0:T(8,128)(2,1)}, u32[]{:S(2)}) copy-start(bf16[1,1024,1024]{2,1,0:T(8,128)(2,1)} %param.11) | copy-start | bytes 6291460
  6.5 61.3 %all-gather.3.cloned.1.call-start = ((), (), s32[]{:S(2)}) async-start(), calls=%async_computation.2 | async-start | bytes 2359296 | tf_op jit(solution)/shard_map/all_gather | solution.py:43
  27.1 130.4 %reduce-scatter.3.cloned.1.call-start = ((), (), s32[]{:S(2)}) async-start(), calls=%async_computation.3 | async-start | bytes 7077888 | tf_op jit(solution)/shard_map/reduce_scatter | solution.py:53
  79.2 191.2 %all-gather.5.cloned.1.call-start = ((), (), s32[]{:S(2)}) async-start(), calls=%async_computation.4 | async-start | bytes 2359296 | tf_op jit(solution)/shard_map/all_gather | solution.py:70
  159.7 22.9 %collective-permute-start = (bf16[127,3072]{1,0:T(8,128)(2,1)}, bf16[127,3072]{1,0:T(8,128)(2,1)}, u32[]{:S(2)}, u32[]{:S(2)}) collective-permute-start(bf16[127,3072]{1,0:T(8,128)(2,1)} %slice.24), channel_id=1, source_target_pairs={{0,8},{8,16},{16,24},{24,32},{32,40},{40,48},{48,56},{1,9},{9,17},... | collective-permute-start | bytes 2340872 | tf_op jit(solution)/shard_map/ppermute | solution.py:13
  177.9 4.6 %copy-start.1 = (bf16[128,3072]{1,0:T(8,128)(2,1)S(1)}, bf16[128,3072]{1,0:T(8,128)(2,1)}, u32[]{:S(2)}) copy-start(bf16[128,3072]{1,0:T(8,128)(2,1)} %reduce-scatter.3.cloned.1.call-done) | copy-start | bytes 2359300
  182.5 1.6 copy-start.3
  206.1 5.4 %copy-start.4 = (bf16[1,128,1024]{2,1,0:T(8,128)(2,1)S(1)}, bf16[1,128,1024]{2,1,0:T(8,128)(2,1)}, u32[]{:S(2)}) copy-start(bf16[1,128,1024]{2,1,0:T(8,128)(2,1)} %param.10) | copy-start | bytes 786436
  209.2 6.5 %collective-permute-start.1 = (bf16[127,1024]{0,1:T(8,128)(2,1)}, bf16[127,1024]{0,1:T(8,128)(2,1)}, u32[]{:S(2)}, u32[]{:S(2)}) collective-permute-start(bf16[127,1024]{0,1:T(8,128)(2,1)} %slice_bitcast_fusion), channel_id=1, source_target_pairs={{0,8},{8,16},{16,24},{24,32},{32,40},{40,48},{48,56},{1,9},{9,17},... | collective-permute-start | bytes 780296 | tf_op jit(solution)/shard_map/ppermute | solution.py:13
  227.1 91.7 %reduce-scatter.5.cloned.1.call-start = ((), (), s32[]{:S(2)}) async-start(), calls=%async_computation.5 | async-start | bytes 2359296 | tf_op jit(solution)/shard_map/reduce_scatter | solution.py:74
  275.7 43.2 %copy-start.2 = (bf16[1,128,1024]{2,1,0:T(8,128)(2,1)S(1)}, bf16[1,128,1024]{2,1,0:T(8,128)(2,1)}, u32[]{:S(2)}) copy-start(bf16[1,128,1024]{2,1,0:T(8,128)(2,1)} %param.6) | copy-start | bytes 786436
  319.8 11.3 %collective-permute-start.2 = (bf16[128,1024]{1,0:T(8,128)(2,1)S(1)}, bf16[128,1024]{1,0:T(8,128)(2,1)S(1)}, u32[]{:S(2)}, u32[]{:S(2)}) collective-permute-start(bf16[128,1024]{1,0:T(8,128)(2,1)S(1)} %fusion.10), channel_id=1, source_target_pairs={{0,64},{64,128},{128,192},{192,0},{1,65},{65,129},{129,193},{193,1... | collective-permute-start | bytes 786440 | tf_op jit(solution)/shard_map/ppermute | solution.py:19
Sparse Core Ops, SparseCore 0:
  27.2 40.6 all-gather.2
  79.3 78.1 reduce-scatter.2
  227.2 43.1 all-gather.4
  275.8 42.9 reduce-scatter.4
where the time goes:
time: 340 us; the launch traced here: 338 us
  waiting for transfers between devices  200 us (59%)
  local copies, waits for them, and re-layouts  42.4 us (12%)
  matrix products  41.3 us (12%)
  blocking collectives  16.8 us (5%)
  between operations  13.2 us (4%)
  starting transfers between devices  12.5 us (4%)
  other arithmetic  11.7 us (3%)
    reduce_scatter x1, waiting for transfers between devices, on_device(): lax.psum_scatter(jnp.dot(gathered, weight_in, preferred_element_type=jnp....  78.2 us
    all_gather x1, waiting for transfers between devices, on_device(): lax.all_gather(gated_out, 'ctx', axis=0, tiled=True)  43.2 us
    reduce_scatter x1, waiting for transfers between devices, on_device(): lax.psum_scatter(partial_value.astype(jnp.bfloat16), 'tp', scatter_dimens...  43.1 us
    all_gather x1, waiting for transfers between devices, on_device(): gathered = lax.all_gather(normed, 'tp', axis=0, tiled=True)  32.1 us
    conv_general_dilated x2, matrix products, causal_mix(): lax.conv_general_dilated(padded[None], kernel, (1,), 'VALID', dimension_n...  24.8 us
    psum x1, blocking collectives, on_device(): squares = lax.psum(jnp.sum(incoming * incoming, axis=1), 'ctx')  16.8 us
    rev x2, local copies, waits for them, and re-layouts, causal_mix(): kernel = tap_weights[::-1][:, None, :]  16 us
    unnamed x14, local copies, waits for them, and re-layouts  12.3 us
  transfers between devices with their start and end apart: 7, of which 6 were waited for; matrix products, arithmetic and copies ran while one was open for 10% of the time, Pallas kernels for 0%

commit v1 on v0

--- a/solution.py
+++ b/solution.py
@@ -67,7 +67,12 @@
     )
     gated_out = (filtered[:, 0] * mixed_sig).astype(jnp.bfloat16)
     partial_value = jnp.dot(
-        lax.all_gather(gated_out, "ctx", axis=0, tiled=True),
+        jnp.concatenate(
+            lax.all_to_all(
+                jnp.stack([gated_out for _ in range(lax.axis_size("ctx"))], 0), "ctx", 0, 0
+            ),
+            axis=0,
+        ),
         weight_out,
         preferred_element_type=jnp.float32,
     )

time: 340 us -> 322 us (0.947)
  waiting for transfers between devices: 200 us -> 154 us
  blocking collectives: 16.8 us -> 47.4 us
    all_gather x1 -> x0, waiting for transfers between devices: 43.2 us -> none  [on_device(): lax.all_gather(gated_out, 'ctx', axis=0, tiled=True)]
    all_to_all x0 -> x1, blocking collectives: none -> 30.7 us  [on_device(): lax.all_to_all(jnp.stack([gated_out for _ in range(lax.axis_size('ctx'))]...]
    unnamed x14 -> x17, local copies, waits for them, and re-layouts: 12.3 us -> 12.2 us
  transfers between devices with their start and end apart: 7 -> 6, of which waited for: 6 -> 5; matrix products, arithmetic and copies ran while one was open for 10% -> 10% of each run, Pallas kernels for 0% -> 0%
where the time goes in v1:
time: 322 us; the launch traced here: 320 us
  waiting for transfers between devices  154 us (48%)
  blocking collectives  47.4 us (15%)
  local copies, waits for them, and re-layouts  42.6 us (13%)
  matrix products  40 us (12%)
  between operations  13.2 us (4%)
  starting transfers between devices  12.5 us (4%)
  other arithmetic  10.2 us (3%)
    reduce_scatter x1, waiting for transfers between devices, on_device(): lax.psum_scatter(jnp.dot(gathered, weight_in, preferred_element_type=jnp....  78.2 us
    reduce_scatter x1, waiting for transfers between devices, on_device(): lax.psum_scatter(partial_value.astype(jnp.bfloat16), 'tp', scatter_dimens...  40.3 us
    all_gather x1, waiting for transfers between devices, on_device(): gathered = lax.all_gather(normed, 'tp', axis=0, tiled=True)  32.1 us
    all_to_all x1, blocking collectives, on_device(): lax.all_to_all(jnp.stack([gated_out for _ in range(lax.axis_size('ctx'))]...  30.7 us
    conv_general_dilated x2, matrix products, causal_mix(): lax.conv_general_dilated(padded[None], kernel, (1,), 'VALID', dimension_n...  25 us
    psum x1, blocking collectives, on_device(): squares = lax.psum(jnp.sum(incoming * incoming, axis=1), 'ctx')  16.8 us
    rev x2, local copies, waits for them, and re-layouts, causal_mix(): kernel = tap_weights[::-1][:, None, :]  16 us
    unnamed x17, local copies, waits for them, and re-layouts  12.2 us
  transfers between devices with their start and end apart: 6, of which 5 were waited for; matrix products, arithmetic and copies ran while one was open for 10% of the time, Pallas kernels for 0%

profile of v1, /device:TPU:1, one launch (start us, length us, event | category | flops | bytes accessed | tf_op | source)
XLA Modules:
  0.0 320.3 jit_solution(2840708281400749232)
XLA Ops:
  6.5 0.8 mul.41
  7.4 1.1 fusion.8
  8.5 16.8 %psum.7 = f32[128]{0:T(128)S(1)} all-reduce(f32[128]{0:T(128)S(1)} %fusion.8), channel_id=1, replica_groups=mesh['pipe'=4,'ctx'=8,'tp'=8] {'ctx'}, use_global_device_ids=true, to_apply=%region_1.0 | all-reduce | flops 128 | bytes 1024 | tf_op jit(solution)/shard_map/psum | solution.py:39
  25.2 1.8 fusion.10
  27.1 8.7 %copy.11 = bf16[1,1024,3,1024]{1,3,2,0:T(8,128)(2,1)} copy(bf16[1,1024,3,1024]{3,1,2,0:T(8,128)(2,1)} %param.8) | data formatting | bytes 12582912 | tf_op args[2]
  35.8 32.1 %all-gather.2.cloned.1.call-done = bf16[1024,1024]{1,0:T(8,128)(2,1)} async-done(((bf16[128,1024]{1,0:T(8,128)(2,1)}), bf16[1024,1024]{1,0:T(8,128)(2,1)}) %all-gather.2.cloned.1.call-update) | async-done | bytes 2097168 | tf_op jit(solution)/shard_map/all_gather | solution.py:43
  67.9 11.2 %convolution_convert_fusion = bf16[1024,3072]{1,0:T(8,128)(2,1)} fusion(bf16[1024,1024]{1,0:T(8,128)(2,1)} %all-gather.2.cloned.1.call-done, bf16[1024,3072]{0,1:T(8,128)(2,1)} %bitcast.43), kind=kOutput, calls=%fused_computation | convolution fusion | flops 6445596672 | bytes 14680064 | tf_op jit(solution)/shard_map/dot_general | solution.py:54
  79.2 78.2 %reduce-scatter.3.cloned.1.call-done = bf16[128,3072]{1,0:T(8,128)(2,1)} async-done(((bf16[1024,3072]{1,0:T(8,128)(2,1)}), bf16[128,3072]{1,0:T(8,128)(2,1)}) %reduce-scatter.3.cloned.1.call-update) | async-done | bytes 786448 | tf_op jit(solution)/shard_map/reduce_scatter | solution.py:53
  157.4 2.2 slice.24
  159.6 2.2 collective-permute-start
  161.8 1.5 copy.12
  163.3 1.3 bitcast_convert_fusion
  164.5 13.3 %rev.6 = f32[128,3072]{0,1:T(8,128)} reverse(f32[128,3072]{0,1:T(8,128)} %bitcast.45), dimensions={0} | reverse | bytes 3145728 | tf_op jit(solution)/shard_map/rev | solution.py:24
  177.9 4.5 %copy.14 = f32[128,1,3072]{2,1,0:T(1,128)} copy(f32[128,1,3072]{0,2,1:T(8,128)} %bitcast.46) | data formatting | bytes 3145728 | tf_op jit(solution)/shard_map/broadcast_in_dim | solution.py:24
  182.5 1.5 maximum_bitcast_fusion
  184.1 17.5 %fusion = f32[1,128,3072]{2,0,1:T(1,128)} fusion(f32[128,1,3072]{2,1,0:T(1,128)S(1)} %copy-done.3, bf16[1,255,3072]{2,1,0:T(8,128)(2,1)S(1)} %maximum_bitcast_fusion), kind=kOutput, calls=%fused_computation.1 | convolution fusion | flops 603979776 | bytes 4712448 | tf_op jit(solution)/shard_map/conv_general_dilated | solution.py:25
  201.6 4.5 %copy.15 = f32[1,128,3072]{1,2,0:T(8,128)} copy(f32[1,128,3072]{2,0,1:T(1,128)} %fusion) | data formatting | bytes 3145728 | tf_op jit(solution)/shard_map/conv_general_dilated | solution.py:25
  206.0 1.5 fusion.14
  207.5 0.8 slice_bitcast_fusion
  208.4 2.3 collective-permute-start.1
  210.7 2.7 rev.7
  213.4 1.1 copy.23
  214.9 1.2 maximum_bitcast_fusion.1
  216.1 2.1 copy.18
  218.2 7.5 %fusion.7 = bf16[1,128,1024]{2,0,1:T(2,128)(2,1)S(1)} fusion(bf16[1,255,1024]{2,0,1:T(2,128)(2,1)} %copy.18, f32[128,1,1024]{2,1,0:T(1,128)} %copy.23, f32[128,1,1024]{2,0,1:T(8,128)S(1)} %bitcast.50), kind=kOutput, calls=%fused_computation.8 | convolution fusion | flops 201588736 | bytes 1832960 | tf_op jit(solution)/shard_map/conv_general_dilated | solution.py:25
  226.1 30.7 %all_to_all.5 = bf16[8,128,1024]{2,1,0:T(8,128)(2,1)S(1)} all-to-all(bf16[8,128,1024]{2,1,0:T(8,128)(2,1)S(1)} %stack.5), channel_id=1, replica_groups=mesh['pipe'=4,'ctx'=8,'tp'=8] {'ctx'}, dimensions={0} | all-to-all | bytes 4194304 | tf_op jit(solution)/shard_map/all_to_all | solution.py:71
  256.7 3.7 %fusion.4 = bf16[1024,1024]{1,0:T(8,128)(2,1)} fusion(bf16[1024,1024]{1,0:T(8,128)(2,1)S(1)} %bitcast.48, bf16[1,1024,1024]{2,1,0:T(8,128)(2,1)S(1)} %copy-done), kind=kOutput, calls=%fused_computation.5 | convolution fusion | flops 2148532224 | bytes 6291456 | tf_op jit(solution)/shard_map/dot_general | solution.py:69
  260.4 40.3 %reduce-scatter.5.cloned.1.call-done = bf16[128,1024]{1,0:T(8,128)(2,1)} async-done(((bf16[1024,1024]{1,0:T(8,128)(2,1)}), bf16[128,1024]{1,0:T(8,128)(2,1)}) %reduce-scatter.5.cloned.1.call-update) | async-done | bytes 262160 | tf_op jit(solution)/shard_map/reduce_scatter | solution.py:79
  300.7 1.0 fusion.11
  301.7 8.0 %collective-permute-start.2 = (bf16[128,1024]{1,0:T(8,128)(2,1)S(1)}, bf16[128,1024]{1,0:T(8,128)(2,1)S(1)}, u32[]{:S(2)}, u32[]{:S(2)}) collective-permute-start(bf16[128,1024]{1,0:T(8,128)(2,1)S(1)} %fusion.11), channel_id=1, source_target_pairs={{0,64},{64,128},{128,192},{192,0},{1,65},{65,129},{129,193},{193,1... | collective-permute-start | bytes 786440 | tf_op jit(solution)/shard_map/ppermute | solution.py:19
  309.7 3.3 %collective-permute-done.2 = bf16[128,1024]{1,0:T(8,128)(2,1)S(1)} collective-permute-done((bf16[128,1024]{1,0:T(8,128)(2,1)S(1)}, bf16[128,1024]{1,0:T(8,128)(2,1)S(1)}, u32[]{:S(2)}, u32[]{:S(2)}) %collective-permute-start.2) | collective-permute-done | bytes 262176 | tf_op jit(solution)/shard_map/ppermute | solution.py:19
  313.1 0.7 copy.31
  (24 shorter events, 1.1 us)
Async XLA Ops:
  6.5 250.2 %copy-start = (bf16[1,1024,1024]{2,1,0:T(8,128)(2,1)S(1)}, bf16[1,1024,1024]{2,1,0:T(8,128)(2,1)}, u32[]{:S(2)}) copy-start(bf16[1,1024,1024]{2,1,0:T(8,128)(2,1)} %param.11) | copy-start | bytes 6291460
  6.5 61.3 %all-gather.2.cloned.1.call-start = ((), (), s32[]{:S(2)}) async-start(), calls=%async_computation.3 | async-start | bytes 2359296 | tf_op jit(solution)/shard_map/all_gather | solution.py:43
  27.1 130.3 %reduce-scatter.3.cloned.1.call-start = ((), (), s32[]{:S(2)}) async-start(), calls=%async_computation.4 | async-start | bytes 7077888 | tf_op jit(solution)/shard_map/reduce_scatter | solution.py:53
  79.1 221.6 %reduce-scatter.5.cloned.1.call-start = ((), (), s32[]{:S(2)}) async-start(), calls=%async_computation.5 | async-start | bytes 2359296 | tf_op jit(solution)/shard_map/reduce_scatter | solution.py:79
  159.6 22.8 %collective-permute-start = (bf16[127,3072]{1,0:T(8,128)(2,1)}, bf16[127,3072]{1,0:T(8,128)(2,1)}, u32[]{:S(2)}, u32[]{:S(2)}) collective-permute-start(bf16[127,3072]{1,0:T(8,128)(2,1)} %slice.24), channel_id=1, source_target_pairs={{0,8},{8,16},{16,24},{24,32},{32,40},{40,48},{48,56},{1,9},{9,17},... | collective-permute-start | bytes 2340872 | tf_op jit(solution)/shard_map/ppermute | solution.py:13
  177.9 4.6 %copy-start.1 = (bf16[128,3072]{1,0:T(8,128)(2,1)S(1)}, bf16[128,3072]{1,0:T(8,128)(2,1)}, u32[]{:S(2)}) copy-start(bf16[128,3072]{1,0:T(8,128)(2,1)} %reduce-scatter.3.cloned.1.call-done) | copy-start | bytes 2359300
  182.4 1.6 copy-start.3
  206.0 4.6 %copy-start.5 = (bf16[1,128,1024]{2,1,0:T(8,128)(2,1)S(1)}, bf16[1,128,1024]{2,1,0:T(8,128)(2,1)}, u32[]{:S(2)}) copy-start(bf16[1,128,1024]{2,1,0:T(8,128)(2,1)} %param.10) | copy-start | bytes 786436
  208.4 6.5 %collective-permute-start.1 = (bf16[127,1024]{0,1:T(8,128)(2,1)}, bf16[127,1024]{0,1:T(8,128)(2,1)}, u32[]{:S(2)}, u32[]{:S(2)}) collective-permute-start(bf16[127,1024]{0,1:T(8,128)(2,1)} %slice_bitcast_fusion), channel_id=1, source_target_pairs={{0,8},{8,16},{16,24},{24,32},{32,40},{40,48},{48,56},{1,9},{9,17},... | collective-permute-start | bytes 780296 | tf_op jit(solution)/shard_map/ppermute | solution.py:13
  214.4 3.7 %copy-start.4 = (f32[128,1024]{1,0:T(8,128)S(1)}, f32[128,1024]{1,0:T(8,128)}, u32[]{:S(2)}) copy-start(f32[128,1024]{1,0:T(8,128)} %rev.7) | copy-start | bytes 1572868
  260.4 40.3 %copy-start.2 = (bf16[1,128,1024]{2,1,0:T(8,128)(2,1)S(1)}, bf16[1,128,1024]{2,1,0:T(8,128)(2,1)}, u32[]{:S(2)}) copy-start(bf16[1,128,1024]{2,1,0:T(8,128)(2,1)} %param.6) | copy-start | bytes 786436
  301.7 11.3 %collective-permute-start.2 = (bf16[128,1024]{1,0:T(8,128)(2,1)S(1)}, bf16[128,1024]{1,0:T(8,128)(2,1)S(1)}, u32[]{:S(2)}, u32[]{:S(2)}) collective-permute-start(bf16[128,1024]{1,0:T(8,128)(2,1)S(1)} %fusion.11), channel_id=1, source_target_pairs={{0,64},{64,128},{128,192},{192,0},{1,65},{65,129},{129,193},{193,1... | collective-permute-start | bytes 786440 | tf_op jit(solution)/shard_map/ppermute | solution.py:19
Sparse Core Ops, SparseCore 0:
  27.2 40.6 all-gather.1
  79.2 78.1 reduce-scatter.2
  260.6 40.1 reduce-scatter.4
